TPU v7x, 32 devices: a whole 2x2x4 slice. The times are simulated.
32 devices in a mesh: mem: 8 (over z, y), lon: 4 (over x, core).
Axes of the slice: x: 2, y: 2, z: 4, core: 2. Of those that a mesh axis runs over, the one named last changes fastest.
Arguments:
- ensemble: float32 [1024, 4, 8192], P('mem', None, 'lon'), may hold values from -6 to 6
- flow_number_field: float32 [4, 8192], P(None, 'lon'), may hold values from -0.9 to 0.9
- obs_index: int32 [32, 512], P(('mem', 'lon')), may hold values from 0 to 1023
- obs_count: int32 [32], P(('mem', 'lon')), may hold values from 128 to 512, as said below
- obs_dist: int32 [32, 512], P(('mem', 'lon')), may hold values from 0 to 31
- observed_readings: float32 [32, 512], P(('mem', 'lon')), may hold values from -6 to 6
- obs_prec: float32 [32, 512], P(('mem', 'lon')), may hold values from 0.5 to 4
Outputs:
- analysis: float32 [1024, 4, 8192], P('mem', None, 'lon')
Inputs may be any that keep to these rules, and one draw needn't show every extreme that they name: `obs_count`: slots from a patch's count on carry no weight; some patch has exactly 512 live slots.
All inputs are finite; a program needn't handle non-finite values. Where the computation divides by a largest or mean magnitude, that divisor is 1e-20 or more.
Results may differ from a plain program's by a relative error of at most 0.002.
The roundings to bfloat16 on the way count: a program that leaves them out, or rounds other values in their place, can miss the bound.
Values sent between devices are 32-bit elements; how exact they have to be, the bound alone decides.
A program may use at most 128 MiB of HBM per device.

v0:
```python
import jax
import jax.numpy as jnp
from jax import lax
from jax.sharding import PartitionSpec as P

highest = lax.Precision.HIGHEST
loc_scale = 12.0


def with_halo(value, sides, width):
    for axis, dim in sides:
        peers, length = (lax.axis_size(axis), value.shape[dim])
        up = [(i, (i + 1) % peers) for i in range(peers)]
        down = [(j, i) for i, j in up]
        last = lax.slice_in_dim(value, length - width, length, axis=dim)
        leading = lax.slice_in_dim(value, 0, width, axis=dim)
        before = lax.ppermute(last, axis, up)
        after = lax.ppermute(leading, axis, down)
        value = jnp.concatenate([before, value, after], axis=dim)
    return value


def donor_cell_advance(haloed_subdomain, flow_number_field):
    centre = haloed_subdomain[..., 1:-1]
    western = haloed_subdomain[..., :-2]
    eastern = haloed_subdomain[..., 2:]
    return (
        centre
        - jnp.maximum(flow_number_field, 0.0) * (centre - western)
        - jnp.minimum(flow_number_field, 0.0) * (eastern - centre)
    )


def analyse(subdomain_slab, obs_cells, live_count, obs_dist, observed_readings, obs_prec):
    members = subdomain_slab.shape[0]
    flat = subdomain_slab.reshape(members, -1)
    column_mean = jnp.mean(flat, axis=0)
    perturb = flat - column_mean
    obs_pert = jnp.take(perturb, obs_cells, axis=1)
    obs_round = obs_pert.astype(jnp.bfloat16)
    slot_total = obs_cells.shape[0]
    slots = jnp.arange(slot_total, dtype=jnp.int32)
    weights = jnp.where(
        slots < live_count,
        obs_prec * jnp.exp(-0.5 * (obs_dist.astype(jnp.float32) / loc_scale) ** 2),
        0.0,
    )
    weighted = (obs_round.astype(jnp.float32) * weights).astype(jnp.bfloat16)
    innovation = observed_readings - jnp.take(column_mean, obs_cells)
    forcing = weights * innovation
    identity = jnp.eye(members, dtype=jnp.float32)
    contract = (((1,), (1,)), ((), ()))
    gram_sum = lax.dot_general(obs_round, weighted, contract, preferred_element_type=jnp.float32)
    drive = jnp.dot(obs_pert, forcing, precision=highest)
    gram = gram_sum + (members - 1.0) * identity
    norm_bound = jnp.max(jnp.sum(jnp.abs(gram), axis=1))
    scaled = gram / norm_bound
    scaled_low = scaled.astype(jnp.bfloat16)
    first_poly = (1.5 * identity - 0.5 * scaled).astype(jnp.bfloat16)
    root_step = jnp.dot(scaled_low, first_poly, preferred_element_type=jnp.float32).astype(
        jnp.bfloat16
    )
    product = jnp.dot(first_poly, root_step, preferred_element_type=jnp.float32)
    second_poly = (1.5 * identity - 0.5 * product).astype(jnp.bfloat16)
    inv_root = jnp.dot(second_poly, first_poly, preferred_element_type=jnp.float32)
    mean_weight = (
        jnp.dot(inv_root, jnp.dot(inv_root, drive, precision=highest), precision=highest)
        / norm_bound
    )
    transform = (mean_weight[:, None] + jnp.sqrt((members - 1.0) / norm_bound) * inv_root).astype(
        jnp.bfloat16
    )
    perturb_low = perturb.astype(jnp.bfloat16)
    applied = lax.dot_general(
        transform, perturb_low, (((0,), (0,)), ((), ())), preferred_element_type=jnp.float32
    )
    result = column_mean + applied
    return result.reshape(subdomain_slab.shape)


def per_device(
    ensemble, flow_number_field, obs_index, obs_count, obs_dist, observed_readings, obs_prec
):
    haloed_subdomain = with_halo(ensemble, (("lon", 2),), 1)
    predicted_member_states = donor_cell_advance(haloed_subdomain, flow_number_field)
    subdomain_slab = lax.all_to_all(
        predicted_member_states, "mem", split_axis=2, concat_axis=0, tiled=True
    )
    analysed = analyse(
        subdomain_slab, obs_index[0], obs_count[0], obs_dist[0], observed_readings[0], obs_prec[0]
    )
    return lax.all_to_all(analysed, "mem", split_axis=0, concat_axis=2, tiled=True)


def solution(mesh):
    placed = (
        P("mem", None, "lon"),
        P(None, "lon"),
        P(("mem", "lon"), None),
        P(("mem", "lon")),
        P(("mem", "lon"), None),
        P(("mem", "lon"), None),
        P(("mem", "lon"), None),
    )
    return jax.shard_map(
        per_device, mesh=mesh, in_specs=placed, out_specs=P("mem", None, "lon"), check_vma=False
    )
```

profile of v0, /device:TPU:29, one launch (start us, length us, event | category | flops | bytes accessed | tf_op | source)
XLA Modules:
  0.0 285.2 jit_solution(11778627437533560661)
XLA Ops:
  0.0 0.0 copy-start.1
  0.0 6.4 %copy.31 = f32[128,4,2048]{0,1,2:T(4,128)} copy(f32[128,4,2048]{2,1,0:T(4,128)} %param.7) | data formatting | bytes 8388608 | tf_op args[0]
  6.4 0.7 fusion.55
  7.1 1.8 collective-permute-start
  8.9 0.0 collective-permute-start.1
  8.9 0.0 copy-done.1
  8.9 0.4 copy.27
  9.2 0.4 copy.32
  9.6 0.0 collective-permute-done
  9.6 2.2 collective-permute-done.1
  11.9 11.7 %fusion.4 = f32[128,4,2048]{0,1,2:T(4,128)} fusion(f32[128,4,2048]{0,1,2:T(4,128)} %copy.31, f32[128,4,1]{0,1,2:T(4,128)S(1)} %collective-permute-done.1, f32[128,4,1]{0,1,2:T(4,128)S(1)} %collective-permute-done, f32[4,2048]{0,1:T(8,128)S(1)} %copy.32, f32[4,2048]{0,1:T(8,128)S(1)} %copy.27), kind=kLoop, calls=%fused_computation.10 | loop fusion | flops 8388608 | bytes 8458240 | tf_op jit(solution)/shard_map/sub | solution.py:28
  23.6 0.0 copy-start.2
  23.6 0.0 copy-start.3
  23.6 0.0 copy-start.4
  23.6 5.6 %all-to-all-start = ((f32[128,4,2048]{0,1,2:T(4,128)}), f32[128,4,2048]{0,1,2:T(4,128)}, u32[]{:S(2)}, u32[]{:S(2)}) async-start(f32[128,4,2048]{0,1,2:T(4,128)} %fusion.4), calls=%async_computation | async-start | bytes 8388608 | tf_op jit(solution)/shard_map/all_to_all | solution.py:86
  29.9 0.0 copy-done.2
  29.9 0.0 copy-done.3
  29.9 0.0 copy-done.4
  30.0 90.7 %all-to-all-done = f32[128,4,2048]{0,1,2:T(4,128)} async-done(((f32[128,4,2048]{0,1,2:T(4,128)}), f32[128,4,2048]{0,1,2:T(4,128)}, u32[]{:S(2)}, u32[]{:S(2)}) %all-to-all-start) | async-done | bytes 4194336 | tf_op jit(solution)/shard_map/all_to_all | solution.py:86
  120.7 5.7 %bitcast_reduce_fusion = f32[4,256]{1,0:T(4,128)S(1)} fusion(f32[128,4,8,256]{0,1,3,2:T(4,128)} %bitcast), kind=kLoop, calls=%fused_computation.15 | loop fusion | flops 1047552 | bytes 4198400 | tf_op jit(solution)/shard_map/reduce_sum | solution.py:37
  126.4 6.6 %copy.36 = f32[128,4,8,256]{0,2,3,1:T(8,128)} copy(f32[128,4,8,256]{0,1,3,2:T(4,128)} %bitcast) | data formatting | bytes 8388608 | tf_op jit(solution)/shard_map/all_to_all | solution.py:86
  133.0 2.3 gather_fusion.1
  135.3 4.9 %bitcast_subtract_fusion = f32[1024,1024]{0,1:T(8,128)} fusion(f32[128,8,8,128]{3,2,1,0:T(8,128)} %bitcast.62, f32[1024]{0:T(1024)S(1)} %bitcast.59), kind=kLoop, calls=%fused_computation.6 | loop fusion | flops 1048576 | bytes 8392704 | tf_op jit(solution)/shard_map/sub | solution.py:38
  140.2 0.0 copy-start.5
  140.2 5.2 %gather_fusion = f32[512,1024]{1,0:T(8,128)S(1)} fusion(f32[1024,1024]{0,1:T(8,128)} %bitcast_subtract_fusion, s32[1024]{0:T(1024)S(1)} %pad_clamp_fusion), kind=kCustom, calls=%fused_computation | custom fusion | bytes 4196352 | tf_op jit(solution)/shard_map/jit(_take)/gather | solution.py:39
  145.4 0.0 copy-done.5
  145.5 1.3 fusion.22
  146.8 3.5 %abs_reduce_fusion = (f32[1024]{0:T(1024)S(1)}, f32[1024,1024]{0,1:T(8,128)}) fusion(f32[512,1024]{1,0:T(8,128)S(1)} %gather_fusion, f32[512]{0:T(512)S(1)} %bitcast.70, pred[512]{0:T(512)(128)(4,1)S(1)} %get-tuple-element.6), kind=kOutput, calls=%fused_computation.17 | convolution fusion | flops 1081605120 | bytes 6298112 | tf_op jit(solution)/shard_map/dot_general | solution.py:53
  150.3 0.6 reduce_max.9
  151.6 9.9 %fusion.1 = bf16[1024,1024]{0,1:T(8,128)(2,1)S(1)} fusion(f32[1024,1024]{0,1:T(8,128)} %get-tuple-element.14, f32[]{:T(128)} %reduce_max.9), kind=kOutput, calls=%fused_computation.5 | convolution fusion | flops 4323278848 | bytes 6291460 | tf_op jit(solution)/shard_map/dot_general | solution.py:63
  161.5 5.2 %fusion.31 = f32[1024,1024]{1,0:T(8,128)S(1)} fusion(bf16[1024,1024]{0,1:T(8,128)(2,1)S(1)} %fusion.1, f32[1024,1024]{0,1:T(8,128)} %get-tuple-element.14, f32[]{:T(128)} %reduce_max.9), kind=kOutput, calls=%fused_computation.37 | convolution fusion | flops 2155872256 | bytes 10485764 | tf_op jit(solution)/shard_map/dot_general | solution.py:65
  166.8 0.0 copy-start
  166.8 3.9 %convolution_bitcast_fusion = f32[1024,1]{0,1:T(1,128)S(1)} fusion(f32[1024,1024]{1,0:T(8,128)S(1)} %fusion.31, f32[1024,1]{0,1:T(1,128)S(1)} %fusion.22), kind=kOutput, calls=%fused_computation.36 | convolution fusion | flops 12582912 | bytes 4202496 | tf_op jit(solution)/shard_map/dot_general | solution.py:67
  170.6 3.7 %fusion.56 = f32[1,1024]{1,0:T(1,128)S(1)} fusion(f32[1024,1024]{1,0:T(8,128)S(1)} %fusion.31, f32[1024,1]{0,1:T(1,128)S(1)} %convolution_bitcast_fusion), kind=kOutput, calls=%fused_computation.66 | convolution fusion | flops 12582912 | bytes 4202496 | tf_op jit(solution)/shard_map/dot_general | solution.py:67
  174.3 0.6 broadcast_divide_fusion
  174.9 0.0 copy-done
  174.9 4.5 %broadcast_add_fusion = f32[1024,1024]{0,1:T(8,128)} fusion(f32[1024]{0:T(1024)S(1)} %bitcast.60, f32[1024,1024]{1,0:T(8,128)S(1)} %fusion.31, f32[]{:T(128)S(6)} %sqrt.3, f32[1024]{0:T(1024)S(1)} %broadcast_divide_fusion, f32[128,8,8,128]{3,2,1,0:T(8,128)S(1)} %bitcast.63), kind=kOutput, calls=%fused_computation.32 | convolution fusion | flops 2153775104 | bytes 12591108 | tf_op jit(solution)/shard_map/dot_general | solution.py:74
  179.4 5.2 %copy.38 = f32[1024,4,256]{2,1,0:T(4,128)} copy(f32[1024,4,256]{0,2,1:T(8,128)} %bitcast.64) | data formatting | bytes 8388608 | tf_op jit(solution)/shard_map/reshape | solution.py:78
  184.7 97.3 %all_to_all.33 = f32[1024,4,256]{2,1,0:T(4,128)S(1)} all-to-all(f32[1024,4,256]{2,1,0:T(4,128)} %copy.38), channel_id=1, replica_groups=mesh['mem'=8,'lon'=4] {'mem'}, dimensions={0} | all-to-all | bytes 8388608 | tf_op jit(solution)/shard_map/all_to_all | solution.py:92
  281.9 3.3 %copy.41 = f32[8,128,1,4,256]{4,3,0,2,1:T(4,128)} copy(f32[8,128,1,4,256]{4,3,2,1,0:T(4,128)S(1)} %bitcast.61) | data formatting | bytes 8388608 | tf_op jit(solution)/shard_map/all_to_all | solution.py:92
  (7 shorter events, 0.1 us)
Async XLA Ops:
  0.0 8.9 %copy-start.1 = (f32[4,2048]{1,0:T(4,128)S(1)}, f32[4,2048]{1,0:T(4,128)}, u32[]{:S(2)}) copy-start(f32[4,2048]{1,0:T(4,128)} %param.8) | copy-start | bytes 98308
  7.1 2.5 collective-permute-start
  8.9 3.0 %collective-permute-start.1 = (f32[128,4,1]{0,1,2:T(4,128)S(1)}, f32[128,4,1]{0,1,2:T(4,128)S(1)}, u32[]{:S(2)}, u32[]{:S(2)}) collective-permute-start(f32[128,4,1]{0,1,2:T(4,128)S(1)} %get-tuple-element.10), channel_id=1, source_target_pairs={{1,0},{2,1},{3,2},{0,3},{5,4},{6,5},{7,6},{4,7},{9,8},{10,9},{11,1... | collective-permute-start | bytes 6152 | tf_op jit(solution)/shard_map/ppermute | solution.py:18
  23.6 6.3 %copy-start.2 = (s32[1,512]{1,0:T(1,128)S(1)}, s32[1,512]{1,0:T(1,128)}, u32[]{:S(2)}) copy-start(s32[1,512]{1,0:T(1,128)} %param.9) | copy-start | bytes 6148
  23.6 6.3 %copy-start.3 = (f32[1,512]{1,0:T(1,128)S(1)}, f32[1,512]{1,0:T(1,128)}, u32[]{:S(2)}) copy-start(f32[1,512]{1,0:T(1,128)} %param.13) | copy-start | bytes 6148
  23.6 6.3 %copy-start.4 = (s32[1,512]{1,0:T(1,128)S(1)}, s32[1,512]{1,0:T(1,128)}, u32[]{:S(2)}) copy-start(s32[1,512]{1,0:T(1,128)} %param.11) | copy-start | bytes 6148
  23.6 97.0 %all-to-all-start = ((f32[128,4,2048]{0,1,2:T(4,128)}), f32[128,4,2048]{0,1,2:T(4,128)}, u32[]{:S(2)}, u32[]{:S(2)}) async-start(f32[128,4,2048]{0,1,2:T(4,128)} %fusion.4), calls=%async_computation | async-start | bytes 8388608 | tf_op jit(solution)/shard_map/all_to_all | solution.py:86
  140.2 5.2 %copy-start.5 = (f32[1,512]{1,0:T(1,128)S(1)}, f32[1,512]{1,0:T(1,128)}, u32[]{:S(2)}) copy-start(f32[1,512]{1,0:T(1,128)} %param.12) | copy-start | bytes 6148
  166.8 8.2 %copy-start = (f32[128,4,8,256]{0,2,3,1:T(8,128)S(1)}, f32[128,4,8,256]{0,2,3,1:T(8,128)}, u32[]{:S(2)}) copy-start(f32[128,4,8,256]{0,2,3,1:T(8,128)} %copy.36) | copy-start | bytes 12582916
where the time goes:
time: 289 us; the launch traced here: 285 us
  blocking collectives  97.3 us (34%)
  waiting for transfers between devices  92.9 us (32%)
  matrix products  32 us (11%)
  local copies, waits for them, and re-layouts  30.5 us (11%)
  other arithmetic  23.7 us (8%)
  starting transfers between devices  7.36 us (3%)
    all_to_all x1, blocking collectives, per_device(): lax.all_to_all(analysed, 'mem', split_axis=0, concat_axis=2, tiled=True)  97.3 us
    all_to_all x1, waiting for transfers between devices, per_device(): lax.all_to_all(predicted_member_states, 'mem', split_axis=2, concat_axis=...  90.7 us
    sub x1, other arithmetic, donor_cell_advance(): centre - jnp.maximum(flow_number_field, 0.0) * (centre - western)  11.7 us
    dot_general x1, matrix products, analyse(): product = jnp.dot(first_poly, root_step, preferred_element_type=jnp.float32)  9.91 us
    all_to_all x1, local copies, waits for them, and re-layouts, per_device(): lax.all_to_all(predicted_member_states, 'mem', split_axis=2, concat_axis=...  6.63 us
    unnamed x14, local copies, waits for them, and re-layouts  6.42 us
  transfers between devices with their start and end apart: 3, of which 2 were waited for; matrix products, arithmetic and copies ran while one was open for 0% of the time, Pallas kernels for 0%

commit v1 on v0

v1 whole, which is shorter than its diff:
```python
import functools
import jax
import jax.numpy as jnp
from jax import lax
from jax.experimental import pallas as pl
from jax.experimental.pallas import tpu as pltpu
from jax.sharding import PartitionSpec as P

loc_scale = 12.0
MESH = pl.DeviceIdType.MESH
f32, bf16 = jnp.float32, jnp.bfloat16


def forecast(ensemble, flow):
    field = jnp.transpose(ensemble, (1, 0, 2))
    peers = lax.axis_size("lon")
    up = [(i, (i + 1) % peers) for i in range(peers)]
    down = [(j, i) for i, j in up]
    before = lax.ppermute(ensemble[..., -1:], "lon", up)
    after = lax.ppermute(ensemble[..., :1], "lon", down)
    before = jnp.transpose(before, (1, 0, 2))
    after = jnp.transpose(after, (1, 0, 2))
    west = jnp.concatenate([before, field[..., :-1]], axis=2)
    east = jnp.concatenate([field[..., 1:], after], axis=2)
    flow = flow[:, None, :]
    return field - jnp.maximum(flow, 0.0) * (field - west) - jnp.minimum(flow, 0.0) * (east - field)


def dot(a, b, dims):
    return lax.dot_general(a, b, (dims, ((), ())), preferred_element_type=f32)


def three_rows(row):
    hi = row.astype(bf16).astype(f32)
    mid = (row - hi).astype(bf16).astype(f32)
    low = row - hi - mid
    which = lax.broadcasted_iota(jnp.int32, (16, row.shape[1]), 0)
    rows = jnp.where(which == 0, hi, jnp.where(which == 1, mid, jnp.where(which == 2, low, 0.0)))
    return rows.astype(bf16)


def as_row(column):
    wide = jnp.broadcast_to(column, (column.shape[0], 128))
    return wide.T[0:1, :]


def kernel(n, fc, cells, weights, readings, out, slab, low, onehot, obs, wtd, big, poly_a, poly_b,
           poly_c, rows, outbuf, send1, recv1, send2, recv2, local):
    levels, members, width = slab.shape
    group = members // n
    me = lax.axis_index("mem")
    total_cells = levels * width
    step = 256
    blocks = members // step

    barrier = pltpu.get_barrier_semaphore()

    def greet(s, _):
        pl.semaphore_signal(barrier, inc=1, device_id={"mem": lax.rem(me + s, n)}, device_id_type=MESH)
        return 0

    lax.fori_loop(1, n, greet, 0)
    pl.semaphore_wait(barrier, n - 1)

    def there(dst, owner):
        return pltpu.make_async_remote_copy(
            src_ref=fc.at[:, :, pl.ds(pl.multiple_of(dst * width, width), width)],
            dst_ref=slab.at[:, pl.ds(pl.multiple_of(owner * group, group), group), :],
            send_sem=send1.at[dst], recv_sem=recv1.at[owner],
            device_id={"mem": dst}, device_id_type=MESH)

    def back(dst, owner):
        return pltpu.make_async_remote_copy(
            src_ref=outbuf.at[:, pl.ds(pl.multiple_of(dst * group, group), group), :],
            dst_ref=out.at[:, :, pl.ds(pl.multiple_of(owner * width, width), width)],
            send_sem=send2.at[dst], recv_sem=recv2.at[owner],
            device_id={"mem": dst}, device_id_type=MESH)

    def go(s, _):
        there(lax.rem(me + s, n), me).start()
        return 0

    lax.fori_loop(1, n, go, 0)
    mine_rows = pl.ds(pl.multiple_of(me * group, group), group)
    mine_columns = pl.ds(pl.multiple_of(me * width, width), width)
    own = pltpu.make_async_copy(fc.at[:, :, mine_columns], slab.at[:, mine_rows, :], local.at[0])
    own.start()

    def fill(b, _):
        at = pl.ds(pl.multiple_of(b * step, step), step)
        cell = lax.broadcasted_iota(jnp.int32, (step, onehot.shape[1]), 0) + b * step
        onehot[at, :] = jnp.where(cell == cells[...], 1.0, 0.0).astype(bf16)
        return 0

    lax.fori_loop(0, total_cells // step, fill, 0)

    def block_sum(src):
        at = pl.ds(pl.multiple_of(src * group, group), group)
        return jnp.concatenate(
            [jnp.sum(slab[l, at, :], axis=0, keepdims=True) for l in range(levels)], axis=1)

    own.wait()

    def gather(s, acc):
        src = lax.rem(me + n - s, n)
        there(src, src).wait_recv()
        return acc + block_sum(src)

    mean = lax.fori_loop(1, n, gather, block_sum(me)) / members
    rows[0:1, :] = mean

    picked = jnp.sum(dot(three_rows(mean), onehot[...], ((1,), (0,))), axis=0, keepdims=True)
    forcing = weights[...] * (readings[...] - picked)
    coef = jnp.sum(dot(three_rows(forcing), onehot[...], ((1,), (1,))), axis=0, keepdims=True)

    def centre(b, _):
        at = pl.ds(pl.multiple_of(b * step, step), step)
        drive = jnp.zeros((step, width), f32)
        for l in range(levels):
            part = slice(l * width, (l + 1) * width)
            p = slab[l, at, :] - mean[:, part]
            low[at, part] = p.astype(bf16)
            drive = drive + p * coef[:, part]
        rows[1:2, at] = as_row(jnp.sum(drive, axis=1, keepdims=True))
        o = dot(low[at, :], onehot[...], ((1,), (0,)))
        obs[at, :] = o.astype(bf16)
        wtd[at, :] = (o.astype(bf16).astype(f32) * weights[...]).astype(bf16)
        return 0

    lax.fori_loop(0, blocks, centre, 0)

    def eye(b):
        r = lax.broadcasted_iota(jnp.int32, (step, members), 0) + b * step
        return r == lax.broadcasted_iota(jnp.int32, (step, members), 1)

    def make_gram(b, bound):
        at = pl.ds(pl.multiple_of(b * step, step), step)
        g = dot(obs[at, :], wtd[...], ((1,), (1,))) + jnp.where(eye(b), members - 1.0, 0.0)
        big[at, :] = g
        sums = jnp.sum(jnp.abs(g), axis=1, keepdims=True)
        return jnp.maximum(bound, jnp.max(sums, axis=0, keepdims=True))

    bound = lax.fori_loop(0, blocks, make_gram, jnp.zeros((1, 1), f32))

    def first(b, _):
        at = pl.ds(pl.multiple_of(b * step, step), step)
        scaled = big[at, :] / bound
        poly_a[at, :] = scaled.astype(bf16)
        poly_b[at, :] = (jnp.where(eye(b), 1.5, 0.0) - 0.5 * scaled).astype(bf16)
        return 0

    lax.fori_loop(0, blocks, first, 0)

    def root(b, _):
        at = pl.ds(pl.multiple_of(b * step, step), step)
        poly_c[at, :] = dot(poly_a[at, :], poly_b[...], ((1,), (0,))).astype(bf16)
        return 0

    lax.fori_loop(0, blocks, root, 0)

    def second(b, _):
        at = pl.ds(pl.multiple_of(b * step, step), step)
        product = dot(poly_b[at, :], poly_c[...], ((1,), (0,)))
        s = (jnp.where(eye(b), 1.5, 0.0) - 0.5 * product).astype(bf16)
        inv = dot(s, poly_b[...], ((1,), (0,)))
        big[at, :] = inv
        rows[2:3, at] = as_row(jnp.sum(inv * rows[1:2, :], axis=1, keepdims=True))
        return 0

    lax.fori_loop(0, blocks, second, 0)
    stretch = jnp.sqrt((members - 1.0) / bound)

    def transform(b, _):
        at = pl.ds(pl.multiple_of(b * step, step), step)
        inv = big[at, :]
        weight = jnp.sum(inv * rows[2:3, :], axis=1, keepdims=True) / bound
        poly_a[at, :] = (weight + stretch * inv).astype(bf16)
        return 0

    lax.fori_loop(0, blocks, transform, 0)

    tile = max(128, group)
    tiles = members // tile
    each = tile // group

    def apply(t, _):
        b = lax.rem(me // each + 1 + t, tiles)
        at = pl.ds(pl.multiple_of(b * tile, tile), tile)
        value = dot(poly_a[:, at], low[...], ((0,), (0,))) + rows[0:1, :]
        for l in range(levels):
            outbuf[l, at, :] = value[:, l * width:(l + 1) * width]
        for g in range(each):
            dst = b * each + g

            @pl.when(dst != me)
            def _():
                back(dst, me).start()
        return 0

    lax.fori_loop(0, tiles, apply, 0)
    own_out = pltpu.make_async_copy(outbuf.at[:, mine_rows, :], out.at[:, :, mine_columns], local.at[1])
    own_out.start()

    def finish(s, _):
        src = lax.rem(me + n - s, n)
        back(src, src).wait_recv()
        back(src, me).wait_send()
        there(src, me).wait_send()
        return 0

    lax.fori_loop(1, n, finish, 0)
    own_out.wait()


def per_device(ensemble, flow, obs_index, obs_count, obs_dist, readings, prec):
    n = lax.axis_size("mem")
    levels = ensemble.shape[1]
    members = ensemble.shape[0] * n
    columns = ensemble.shape[2]
    width = columns // n
    cells, slots = levels * width, obs_index.shape[1]
    fc = forecast(ensemble, flow)
    live = lax.broadcasted_iota(jnp.int32, (1, slots), 1) < obs_count[0]
    weights = jnp.where(live, prec * jnp.exp(-0.5 * (obs_dist.astype(f32) / loc_scale) ** 2), 0.0)
    vmem = pl.BlockSpec(memory_space=pltpu.VMEM)
    hbm = pl.BlockSpec(memory_space=pl.ANY)
    result = pl.pallas_call(
        functools.partial(kernel, n),
        out_shape=jax.ShapeDtypeStruct(fc.shape, f32),
        in_specs=[hbm, vmem, vmem, vmem],
        out_specs=hbm,
        scratch_shapes=[
            pltpu.VMEM((levels, members, width), f32),
            pltpu.VMEM((members, cells), bf16),
            pltpu.VMEM((cells, slots), bf16),
            pltpu.VMEM((members, slots), bf16),
            pltpu.VMEM((members, slots), bf16),
            pltpu.VMEM((members, members), f32),
            pltpu.VMEM((members, members), bf16),
            pltpu.VMEM((members, members), bf16),
            pltpu.VMEM((members, members), bf16),
            pltpu.VMEM((8, max(members, cells)), f32),
            pltpu.VMEM((levels, members, width), f32),
            pltpu.SemaphoreType.DMA((n,)),
            pltpu.SemaphoreType.DMA((n,)),
            pltpu.SemaphoreType.DMA((n,)),
            pltpu.SemaphoreType.DMA((n,)),
            pltpu.SemaphoreType.DMA((2,)),
        ],
        compiler_params=pltpu.CompilerParams(
            collective_id=0, has_side_effects=True, vmem_limit_bytes=60 * 1024 * 1024),
        name="regroup_analyse",
    )(fc, obs_index, weights, readings)
    return jnp.transpose(result, (1, 0, 2))


def solution(mesh):
    placed = (
        P("mem", None, "lon"),
        P(None, "lon"),
        P(("mem", "lon"), None),
        P(("mem", "lon")),
        P(("mem", "lon"), None),
        P(("mem", "lon"), None),
        P(("mem", "lon"), None),
    )
    return jax.shard_map(
        per_device, mesh=mesh, in_specs=placed, out_specs=P("mem", None, "lon"), check_vma=False
    )
```

time: 289 us -> 238 us (0.82); the launches traced: 285 us -> 238 us
  Pallas kernels: 0 us -> 213 us
  blocking collectives: 97.3 us -> 0 us
  waiting for transfers between devices: 92.9 us -> 0.01 us
  matrix products: 32 us -> 0 us
  other arithmetic: 23.7 us -> 7.2 us
  local copies, waits for them, and re-layouts: 30.5 us -> 14.6 us
  starting transfers between devices: 7.36 us -> 1.88 us
    pallas_call x0 -> x1, Pallas kernels: none -> 213 us  [per_device(): pl.pallas_call(functools.partial(kernel, n), out_shape=jax.ShapeDtypeStru...]
    all_to_all x1 -> x0, blocking collectives: 97.3 us -> none  [per_device(): lax.all_to_all(analysed, 'mem', split_axis=0, concat_axis=2, tiled=True)]
    all_to_all x1 -> x0, waiting for transfers between devices: 90.7 us -> none  [per_device(): lax.all_to_all(predicted_member_states, 'mem', split_axis=2, concat_axis=...]
    dot_general x7 -> x0, matrix products: 32 us -> none  [the longest x1 9.91 us: analyse(): product = jnp.dot(first_poly, root_step, preferred_element_type=jnp.float32)]
    sub x2 -> x1, other arithmetic: 16.6 us -> 6.6 us  [forecast(): field - jnp.maximum(flow, 0.0) * (field - west)]
    all_to_all x2 -> x0, local copies, waits for them, and re-layouts: 9.88 us -> none  [the longest x1 6.63 us: per_device(): lax.all_to_all(predicted_member_states, 'mem', split_axis=2, concat_axis=...]
    gather x2 -> x0, local copies, waits for them, and re-layouts: 7.48 us -> none  [the longest x1 5.2 us: analyse(): obs_pert = jnp.take(perturb, obs_cells, axis=1)]
    transpose x0 -> x1, local copies, waits for them, and re-layouts: none -> 6.9 us  [per_device(): return jnp.transpose(result, (1, 0, 2))]
  transfers between devices with their start and end apart: 3 -> 2, of which waited for: 2 -> 0; matrix products, arithmetic and copies ran while one was open for 0% -> 3% of each run, Pallas kernels for 0% -> 0%
where the time goes in v1:
time: 238 us
  Pallas kernels  213 us (89%)
  local copies, waits for them, and re-layouts  14.6 us (6%)
  other arithmetic  7.2 us (3%)
    pallas_call x1, Pallas kernels, per_device(): pl.pallas_call(functools.partial(kernel, n), out_shape=jax.ShapeDtypeStru...  213 us
    transpose x1, local copies, waits for them, and re-layouts, per_device(): return jnp.transpose(result, (1, 0, 2))  6.9 us
    sub x1, other arithmetic, forecast(): field - jnp.maximum(flow, 0.0) * (field - west)  6.6 us
  transfers between devices with their start and end apart: 2, of which 0 were waited for; matrix products, arithmetic and copies ran while one was open for 3% of the time, Pallas kernels for 0%

profile of v1, /device:TPU:29, one launch (start us, length us, event | category | flops | bytes accessed | tf_op | source)
XLA Modules:
  0.0 237.7 jit_solution(17175152851433375685)
XLA Ops:
  0.0 1.2 fusion.5
  1.3 1.8 collective-permute-start
  3.1 0.1 collective-permute-start.1
  3.2 4.6 %copy.16 = f32[128,4,2048]{2,0,1:T(8,128)S(1)} copy(f32[128,4,2048]{2,1,0:T(4,128)} %param.7) | data formatting | bytes 8388608 | tf_op args[0]
  7.8 0.0 copy-start.1
  7.8 0.0 copy-start.2
  7.8 0.0 copy-start.3
  7.8 0.0 copy-start
  7.8 1.7 fusion.4
  9.6 0.0 copy-done.1
  10.3 0.0 copy-done.2
  10.3 0.0 copy-done.3
  10.3 0.6 compare_select_fusion.weights
  10.9 0.0 collective-permute-done
  10.9 0.0 collective-permute-done.1
  10.9 0.0 copy-done
  10.9 6.6 %fusion.2.fc = f32[4,128,2048]{2,1,0:T(8,128)} fusion(f32[4,128,2047]{2,1,0:T(8,128)S(1)} %get-tuple-element.6, f32[4,128,1]{2,1,0:T(8,128)S(1)} %bitcast.11, f32[4,128,1]{2,1,0:T(8,128)S(1)} %bitcast.12, f32[4,128,2047]{2,1,0:T(8,128)S(1)} %get-tuple-element.5, f32[4,2048]{1,0:T(4,128)S(1)} %get-tuple-element.10, f32[4,2048]{1,0:T(4,128)S(1)} %get-tuple-element.9, ...), kind=kLoop, calls=%fused_computation.3 | loop fusion | flops 8388608 | bytes 16842752 | tf_op jit(solution)/shard_map/sub | solution.py:26
  17.5 213.3 %regroup_analyse.1 = f32[4,128,2048]{2,1,0:T(8,128)} custom-call(f32[4,128,2048]{2,1,0:T(8,128)} %fusion.2.fc, s32[1,512]{1,0:T(1,128)} %cells.1, f32[1,512]{1,0:T(1,128)} %compare_select_fusion.weights, f32[1,512]{1,0:T(1,128)} %readings.1), custom_call_target="tpu_custom_call" | custom-call | tf_op jit(solution)/shard_map/regroup_analyse/pallas_call | solution.py:227
  230.8 6.9 %copy.11 = f32[128,4,2048]{2,1,0:T(4,128)} copy(f32[128,4,2048]{2,0,1:T(8,128)} %bitcast.10) | data formatting | bytes 8388608 | tf_op jit(solution)/shard_map/transpose | solution.py:254
  (3 shorter events, 0.1 us)
Async XLA Ops:
  1.3 9.6 %collective-permute-start = (f32[128,4,1]{2,0,1:T(8,128)S(1)}, f32[128,4,1]{2,0,1:T(8,128)S(1)}, u32[]{:S(2)}, u32[]{:S(2)}) collective-permute-start(f32[128,4,1]{2,0,1:T(8,128)S(1)} %copy.14), channel_id=1, source_target_pairs={{0,1},{1,2},{2,3},{3,0},{4,5},{5,6},{6,7},{7,4},{8,9},{9,10},{10,1... | collective-permute-start | bytes 6152 | tf_op jit(solution)/shard_map/ppermute | solution.py:19
  3.1 7.8 %collective-permute-start.1 = (f32[128,4,1]{2,0,1:T(8,128)S(1)}, f32[128,4,1]{2,0,1:T(8,128)S(1)}, u32[]{:S(2)}, u32[]{:S(2)}) collective-permute-start(f32[128,4,1]{2,0,1:T(8,128)S(1)} %copy.15), channel_id=1, source_target_pairs={{1,0},{2,1},{3,2},{0,3},{5,4},{6,5},{7,6},{4,7},{9,8},{10,9},{11,1... | collective-permute-start | bytes 6152 | tf_op jit(solution)/shard_map/ppermute | solution.py:20
  7.8 1.8 copy-start.1
  7.8 2.5 %copy-start.2 = (f32[1,512]{1,0:T(1,128)S(1)}, f32[1,512]{1,0:T(1,128)}, u32[]{:S(2)}) copy-start(f32[1,512]{1,0:T(1,128)} %param.13) | copy-start | bytes 6148
  7.8 2.5 %copy-start.3 = (s32[1,512]{1,0:T(1,128)S(1)}, s32[1,512]{1,0:T(1,128)}, u32[]{:S(2)}) copy-start(s32[1,512]{1,0:T(1,128)} %param.11) | copy-start | bytes 6148
  7.8 3.0 %copy-start = (f32[128,4,2048]{2,1,0:T(4,128)S(1)}, f32[128,4,2048]{2,1,0:T(4,128)}, u32[]{:S(2)}) copy-start(f32[128,4,2048]{2,1,0:T(4,128)} %param.7) | copy-start | bytes 12582916

commit v2 on v1

--- a/solution.py
+++ b/solution.py
@@ -45,7 +45,7 @@
 
 
 def kernel(n, fc, cells, weights, readings, out, slab, low, onehot, obs, wtd, big, poly_a, poly_b,
-           poly_c, rows, outbuf, send1, recv1, send2, recv2, local):
+           poly_c, rows, outbuf, send1, recv1, send2, recv2, local, gate):
     levels, members, width = slab.shape
     group = members // n
     me = lax.axis_index("mem")
@@ -53,14 +53,20 @@
     step = 256
     blocks = members // step
 
+    lon = lax.axis_index("lon")
+    paired = lax.axis_size("lon") % 2 == 0
+    second_of_pair = lax.rem(lon, 2) == 1
+    partner = lon + 1 - 2 * lax.rem(lon, 2)
     barrier = pltpu.get_barrier_semaphore()
+    if paired:
+        pl.semaphore_signal(barrier, inc=1, device_id={"lon": partner}, device_id_type=MESH)
 
     def greet(s, _):
         pl.semaphore_signal(barrier, inc=1, device_id={"mem": lax.rem(me + s, n)}, device_id_type=MESH)
         return 0
 
     lax.fori_loop(1, n, greet, 0)
-    pl.semaphore_wait(barrier, n - 1)
+    pl.semaphore_wait(barrier, n if paired else n - 1)
 
     def there(dst, owner):
         return pltpu.make_async_remote_copy(
@@ -80,6 +86,12 @@
         there(lax.rem(me + s, n), me).start()
         return 0
 
+    if paired:
+
+        @pl.when(second_of_pair)
+        def _():
+            pl.semaphore_wait(gate, 1)
+
     lax.fori_loop(1, n, go, 0)
     mine_rows = pl.ds(pl.multiple_of(me * group, group), group)
     mine_columns = pl.ds(pl.multiple_of(me * width, width), width)
@@ -93,6 +105,17 @@
         return 0
 
     lax.fori_loop(0, total_cells // step, fill, 0)
+
+    def sent(s, _):
+        there(lax.rem(me + s, n), me).wait_send()
+        return 0
+
+    lax.fori_loop(1, n, sent, 0)
+    if paired:
+
+        @pl.when(jnp.logical_not(second_of_pair))
+        def _():
+            pl.semaphore_signal(gate, inc=1, device_id={"lon": partner}, device_id_type=MESH)
 
     def block_sum(src):
         at = pl.ds(pl.multiple_of(src * group, group), group)
@@ -205,7 +228,6 @@
         src = lax.rem(me + n - s, n)
         back(src, src).wait_recv()
         back(src, me).wait_send()
-        there(src, me).wait_send()
         return 0
 
     lax.fori_loop(1, n, finish, 0)
@@ -246,6 +268,7 @@
             pltpu.SemaphoreType.DMA((n,)),
             pltpu.SemaphoreType.DMA((n,)),
             pltpu.SemaphoreType.DMA((2,)),
+            pltpu.SemaphoreType.REGULAR,
         ],
         compiler_params=pltpu.CompilerParams(
             collective_id=0, has_side_effects=True, vmem_limit_bytes=60 * 1024 * 1024),

time: 238 us -> 228 us (0.958)
  Pallas kernels: 213 us -> 203 us
    pallas_call x1, Pallas kernels: 213 us -> 203 us  [per_device(): pl.pallas_call(functools.partial(kernel, n), out_shape=jax.ShapeDtypeStru...]
where the time goes in v2:
time: 228 us; the launch traced here: 227 us
  Pallas kernels  203 us (89%)
  local copies, waits for them, and re-layouts  14.5 us (6%)
  other arithmetic  7.02 us (3%)
    pallas_call x1, Pallas kernels, per_device(): pl.pallas_call(functools.partial(kernel, n), out_shape=jax.ShapeDtypeStru...  203 us
    transpose x1, local copies, waits for them, and re-layouts, per_device(): return jnp.transpose(result, (1, 0, 2))  6.9 us
    sub x1, other arithmetic, forecast(): field - jnp.maximum(flow, 0.0) * (field - west)  6.42 us
    unnamed x11, local copies, waits for them, and re-layouts  4.68 us
  transfers between devices with their start and end apart: 2, of which 0 were waited for; matrix products, arithmetic and copies ran while one was open for 3% of the time, Pallas kernels for 0%

profile of v2, /device:TPU:29, one launch (start us, length us, event | category | flops | bytes accessed | tf_op | source)
XLA Modules:
  0.0 227.2 jit_solution(17614267429996232449)
XLA Ops:
  0.0 1.2 fusion.5
  1.3 1.8 collective-permute-start
  3.1 0.1 collective-permute-start.1
  3.2 4.6 %copy.16 = f32[128,4,2048]{2,0,1:T(8,128)S(1)} copy(f32[128,4,2048]{2,1,0:T(4,128)} %param.7) | data formatting | bytes 8388608 | tf_op args[0]
  7.8 0.0 copy-start.1
  7.8 0.0 copy-start.2
  7.8 0.0 copy-start.3
  7.8 0.0 copy-start
  7.8 1.7 fusion.4
  9.6 0.0 copy-done.1
  10.3 0.0 copy-done.2
  10.3 0.0 copy-done.3
  10.3 0.6 compare_select_fusion.weights
  10.9 0.0 collective-permute-done
  10.9 0.0 collective-permute-done.1
  10.9 0.0 copy-done
  10.9 6.4 %fusion.2.fc = f32[4,128,2048]{2,1,0:T(8,128)} fusion(f32[4,128,2047]{2,1,0:T(8,128)S(1)} %get-tuple-element.6, f32[4,128,1]{2,1,0:T(8,128)S(1)} %bitcast.11, f32[4,128,1]{2,1,0:T(8,128)S(1)} %bitcast.12, f32[4,128,2047]{2,1,0:T(8,128)S(1)} %get-tuple-element.5, f32[4,2048]{1,0:T(4,128)S(1)} %get-tuple-element.10, f32[4,2048]{1,0:T(4,128)S(1)} %get-tuple-element.9, ...), kind=kLoop, calls=%fused_computation.3 | loop fusion | flops 8388608 | bytes 16842752 | tf_op jit(solution)/shard_map/sub | solution.py:26
  17.3 203.0 %regroup_analyse.1 = f32[4,128,2048]{2,1,0:T(8,128)} custom-call(f32[4,128,2048]{2,1,0:T(8,128)} %fusion.2.fc, s32[1,512]{1,0:T(1,128)} %cells.1, f32[1,512]{1,0:T(1,128)} %compare_select_fusion.weights, f32[1,512]{1,0:T(1,128)} %readings.1), custom_call_target="tpu_custom_call" | custom-call | tf_op jit(solution)/shard_map/regroup_analyse/pallas_call | solution.py:249
  220.3 6.9 %copy.11 = f32[128,4,2048]{2,1,0:T(4,128)} copy(f32[128,4,2048]{2,0,1:T(8,128)} %bitcast.10) | data formatting | bytes 8388608 | tf_op jit(solution)/shard_map/transpose | solution.py:277
  (3 shorter events, 0.1 us)
Async XLA Ops:
  1.3 9.6 %collective-permute-start = (f32[128,4,1]{2,0,1:T(8,128)S(1)}, f32[128,4,1]{2,0,1:T(8,128)S(1)}, u32[]{:S(2)}, u32[]{:S(2)}) collective-permute-start(f32[128,4,1]{2,0,1:T(8,128)S(1)} %copy.14), channel_id=1, source_target_pairs={{0,1},{1,2},{2,3},{3,0},{4,5},{5,6},{6,7},{7,4},{8,9},{9,10},{10,1... | collective-permute-start | bytes 6152 | tf_op jit(solution)/shard_map/ppermute | solution.py:19
  3.1 7.8 %collective-permute-start.1 = (f32[128,4,1]{2,0,1:T(8,128)S(1)}, f32[128,4,1]{2,0,1:T(8,128)S(1)}, u32[]{:S(2)}, u32[]{:S(2)}) collective-permute-start(f32[128,4,1]{2,0,1:T(8,128)S(1)} %copy.15), channel_id=1, source_target_pairs={{1,0},{2,1},{3,2},{0,3},{5,4},{6,5},{7,6},{4,7},{9,8},{10,9},{11,1... | collective-permute-start | bytes 6152 | tf_op jit(solution)/shard_map/ppermute | solution.py:20
  7.8 1.8 copy-start.1
  7.8 2.5 %copy-start.2 = (f32[1,512]{1,0:T(1,128)S(1)}, f32[1,512]{1,0:T(1,128)}, u32[]{:S(2)}) copy-start(f32[1,512]{1,0:T(1,128)} %param.13) | copy-start | bytes 6148
  7.8 2.5 %copy-start.3 = (s32[1,512]{1,0:T(1,128)S(1)}, s32[1,512]{1,0:T(1,128)}, u32[]{:S(2)}) copy-start(s32[1,512]{1,0:T(1,128)} %param.11) | copy-start | bytes 6148
  7.8 3.0 %copy-start = (f32[128,4,2048]{2,1,0:T(4,128)S(1)}, f32[128,4,2048]{2,1,0:T(4,128)}, u32[]{:S(2)}) copy-start(f32[128,4,2048]{2,1,0:T(4,128)} %param.7) | copy-start | bytes 12582916

commit v3 on v2

--- a/solution.py
+++ b/solution.py
@@ -11,21 +11,6 @@
 f32, bf16 = jnp.float32, jnp.bfloat16
 
 
-def forecast(ensemble, flow):
-    field = jnp.transpose(ensemble, (1, 0, 2))
-    peers = lax.axis_size("lon")
-    up = [(i, (i + 1) % peers) for i in range(peers)]
-    down = [(j, i) for i, j in up]
-    before = lax.ppermute(ensemble[..., -1:], "lon", up)
-    after = lax.ppermute(ensemble[..., :1], "lon", down)
-    before = jnp.transpose(before, (1, 0, 2))
-    after = jnp.transpose(after, (1, 0, 2))
-    west = jnp.concatenate([before, field[..., :-1]], axis=2)
-    east = jnp.concatenate([field[..., 1:], after], axis=2)
-    flow = flow[:, None, :]
-    return field - jnp.maximum(flow, 0.0) * (field - west) - jnp.minimum(flow, 0.0) * (east - field)
-
-
 def dot(a, b, dims):
     return lax.dot_general(a, b, (dims, ((), ())), preferred_element_type=f32)
 
@@ -44,47 +29,98 @@
     return wide.T[0:1, :]
 
 
-def kernel(n, fc, cells, weights, readings, out, slab, low, onehot, obs, wtd, big, poly_a, poly_b,
-           poly_c, rows, outbuf, send1, recv1, send2, recv2, local, gate):
+def kernel(n, ens, flow, cells, count, dist, prec, readings, out, field, slab, low, onehot, obs, wtd, big,
+           poly_a, poly_b, poly_c, rows, outbuf, backbuf, edges, loads, stores, send1, recv1, send2, recv2,
+           local, gate):
     levels, members, width = slab.shape
     group = members // n
+    columns = n * width
+    pad = 128
     me = lax.axis_index("mem")
     total_cells = levels * width
     step = 256
     blocks = members // step
-
-    lon = lax.axis_index("lon")
-    paired = lax.axis_size("lon") % 2 == 0
+    lon, peers = lax.axis_index("lon"), lax.axis_size("lon")
+    lon_east, lon_west = lax.rem(lon + 1, peers), lax.rem(lon + peers - 1, peers)
+    paired = peers % 2 == 0
     second_of_pair = lax.rem(lon, 2) == 1
     partner = lon + 1 - 2 * lax.rem(lon, 2)
+
+    inputs = [pltpu.make_async_copy(ens.at[:, l, :], field.at[l, :, pad:pad + columns], loads.at[l])
+              for l in range(levels)]
+    for load in inputs:
+        load.start()
+
     barrier = pltpu.get_barrier_semaphore()
-    if paired:
-        pl.semaphore_signal(barrier, inc=1, device_id={"lon": partner}, device_id_type=MESH)
+    for side in (lon_east, lon_west):
+        pl.semaphore_signal(barrier, inc=1, device_id={"lon": side}, device_id_type=MESH)
 
     def greet(s, _):
         pl.semaphore_signal(barrier, inc=1, device_id={"mem": lax.rem(me + s, n)}, device_id_type=MESH)
         return 0
 
     lax.fori_loop(1, n, greet, 0)
-    pl.semaphore_wait(barrier, n if paired else n - 1)
+    pl.semaphore_wait(barrier, n + 1)
+
+    halo = []
+    for l in range(levels):
+        for side, (dst, take, put) in enumerate((
+                (lon_east, columns - pad, 0), (lon_west, 0, pad + columns))):
+            halo.append(pltpu.make_async_remote_copy(
+                src_ref=ens.at[:, l, take:take + pad], dst_ref=field.at[l, :, put:put + pad],
+                send_sem=edges.at[0, side, l], recv_sem=edges.at[1, side, l],
+                device_id={"lon": dst}, device_id_type=MESH))
+    for edge in halo:
+        edge.start()
+
+    def rows_of(device):
+        return pl.ds(pl.multiple_of(device * group, group), group)
+
+    def columns_of(device):
+        return pl.ds(pl.multiple_of(device * width, width), width)
 
     def there(dst, owner):
         return pltpu.make_async_remote_copy(
-            src_ref=fc.at[:, :, pl.ds(pl.multiple_of(dst * width, width), width)],
-            dst_ref=slab.at[:, pl.ds(pl.multiple_of(owner * group, group), group), :],
+            src_ref=outbuf.at[:, rows_of(dst), :], dst_ref=slab.at[:, rows_of(owner), :],
             send_sem=send1.at[dst], recv_sem=recv1.at[owner],
             device_id={"mem": dst}, device_id_type=MESH)
 
     def back(dst, owner):
         return pltpu.make_async_remote_copy(
-            src_ref=outbuf.at[:, pl.ds(pl.multiple_of(dst * group, group), group), :],
-            dst_ref=out.at[:, :, pl.ds(pl.multiple_of(owner * width, width), width)],
+            src_ref=outbuf.at[:, rows_of(dst), :], dst_ref=backbuf.at[:, rows_of(owner), :],
             send_sem=send2.at[dst], recv_sem=recv2.at[owner],
             device_id={"mem": dst}, device_id_type=MESH)
 
-    def go(s, _):
-        there(lax.rem(me + s, n), me).start()
-        return 0
+    def place(owner):
+        return [pltpu.make_async_copy(
+            backbuf.at[l, rows_of(owner), :], out.at[:, l, columns_of(owner)], stores.at[owner, l])
+            for l in range(levels)]
+
+    def advance(dst):
+        for l in range(levels):
+            value = field[l, :, pl.ds(pl.multiple_of(dst * width, 128), width + 2 * pad)]
+            span = width + 2 * pad
+            west = pltpu.roll(value, 1, 1)[:, pad:pad + width]
+            east = pltpu.roll(value, span - 1, 1)[:, pad:pad + width]
+            centre = value[:, pad:pad + width]
+            f = flow[l:l + 1, columns_of(dst)]
+            outbuf[l, rows_of(dst), :] = (
+                centre - jnp.maximum(f, 0.0) * (centre - west) - jnp.minimum(f, 0.0) * (east - centre))
+
+    own = pltpu.make_async_copy(outbuf.at[:, rows_of(me), :], slab.at[:, rows_of(me), :], local.at[0])
+    for load in inputs:
+        load.wait()
+
+    def send_forecast(dst):
+        advance(dst)
+
+        @pl.when(dst != me)
+        def _():
+            there(dst, me).start()
+
+        @pl.when(dst == me)
+        def _():
+            own.start()
 
     if paired:
 
@@ -92,11 +128,19 @@
         def _():
             pl.semaphore_wait(gate, 1)
 
-    lax.fori_loop(1, n, go, 0)
-    mine_rows = pl.ds(pl.multiple_of(me * group, group), group)
-    mine_columns = pl.ds(pl.multiple_of(me * width, width), width)
-    own = pltpu.make_async_copy(fc.at[:, :, mine_columns], slab.at[:, mine_rows, :], local.at[0])
-    own.start()
+    def inner(s, _):
+        send_forecast(1 + lax.rem(me + s, n - 2))
+        return 0
+
+    lax.fori_loop(0, n - 2, inner, 0)
+    for edge in halo:
+        edge.wait()
+
+    def outer(s, _):
+        send_forecast(s * (n - 1))
+        return 0
+
+    lax.fori_loop(0, 2, outer, 0)
 
     def fill(b, _):
         at = pl.ds(pl.multiple_of(b * step, step), step)
@@ -105,6 +149,9 @@
         return 0
 
     lax.fori_loop(0, total_cells // step, fill, 0)
+    live = lax.broadcasted_iota(jnp.int32, cells.shape, 1) < count[...]
+    reach = prec[...] * jnp.exp(-0.5 * (dist[...].astype(f32) / loc_scale) ** 2)
+    weights = jnp.where(live, reach, 0.0)
 
     def sent(s, _):
         there(lax.rem(me + s, n), me).wait_send()
@@ -133,7 +180,7 @@
     rows[0:1, :] = mean
 
     picked = jnp.sum(dot(three_rows(mean), onehot[...], ((1,), (0,))), axis=0, keepdims=True)
-    forcing = weights[...] * (readings[...] - picked)
+    forcing = weights * (readings[...] - picked)
     coef = jnp.sum(dot(three_rows(forcing), onehot[...], ((1,), (1,))), axis=0, keepdims=True)
 
     def centre(b, _):
@@ -147,7 +194,7 @@
         rows[1:2, at] = as_row(jnp.sum(drive, axis=1, keepdims=True))
         o = dot(low[at, :], onehot[...], ((1,), (0,)))
         obs[at, :] = o.astype(bf16)
-        wtd[at, :] = (o.astype(bf16).astype(f32) * weights[...]).astype(bf16)
+        wtd[at, :] = (o.astype(bf16).astype(f32) * weights).astype(bf16)
         return 0
 
     lax.fori_loop(0, blocks, centre, 0)
@@ -221,60 +268,73 @@
         return 0
 
     lax.fori_loop(0, tiles, apply, 0)
-    own_out = pltpu.make_async_copy(outbuf.at[:, mine_rows, :], out.at[:, :, mine_columns], local.at[1])
-    own_out.start()
-
-    def finish(s, _):
+    backbuf[:, rows_of(me), :] = outbuf[:, rows_of(me), :]
+    for put in place(me):
+        put.start()
+
+    def arrive(s, _):
         src = lax.rem(me + n - s, n)
         back(src, src).wait_recv()
-        back(src, me).wait_send()
+        for put in place(src):
+            put.start()
+        return 0
+
+    lax.fori_loop(1, n, arrive, 0)
+
+    def finish(s, _):
+        dst = lax.rem(me + n - s, n)
+        back(dst, me).wait_send()
+        for put in place(dst):
+            put.wait()
         return 0
 
     lax.fori_loop(1, n, finish, 0)
-    own_out.wait()
+    for put in place(me):
+        put.wait()
 
 
 def per_device(ensemble, flow, obs_index, obs_count, obs_dist, readings, prec):
     n = lax.axis_size("mem")
-    levels = ensemble.shape[1]
-    members = ensemble.shape[0] * n
-    columns = ensemble.shape[2]
-    width = columns // n
+    group, levels, columns = ensemble.shape
+    members, width = group * n, columns // n
     cells, slots = levels * width, obs_index.shape[1]
-    fc = forecast(ensemble, flow)
-    live = lax.broadcasted_iota(jnp.int32, (1, slots), 1) < obs_count[0]
-    weights = jnp.where(live, prec * jnp.exp(-0.5 * (obs_dist.astype(f32) / loc_scale) ** 2), 0.0)
     vmem = pl.BlockSpec(memory_space=pltpu.VMEM)
     hbm = pl.BlockSpec(memory_space=pl.ANY)
-    result = pl.pallas_call(
+    slab = pltpu.VMEM((levels, members, width), f32)
+    square = pltpu.VMEM((members, members), bf16)
+    return pl.pallas_call(
         functools.partial(kernel, n),
-        out_shape=jax.ShapeDtypeStruct(fc.shape, f32),
-        in_specs=[hbm, vmem, vmem, vmem],
+        out_shape=jax.ShapeDtypeStruct(ensemble.shape, f32),
+        in_specs=[hbm] + [vmem] * 6,
         out_specs=hbm,
         scratch_shapes=[
-            pltpu.VMEM((levels, members, width), f32),
+            pltpu.VMEM((levels, group, columns + 256), f32),
+            slab,
             pltpu.VMEM((members, cells), bf16),
             pltpu.VMEM((cells, slots), bf16),
             pltpu.VMEM((members, slots), bf16),
             pltpu.VMEM((members, slots), bf16),
             pltpu.VMEM((members, members), f32),
-            pltpu.VMEM((members, members), bf16),
-            pltpu.VMEM((members, members), bf16),
-            pltpu.VMEM((members, members), bf16),
+            square,
+            square,
+            square,
             pltpu.VMEM((8, max(members, cells)), f32),
-            pltpu.VMEM((levels, members, width), f32),
+            slab,
+            slab,
+            pltpu.SemaphoreType.DMA((2, 2, levels)),
+            pltpu.SemaphoreType.DMA((levels,)),
+            pltpu.SemaphoreType.DMA((n, levels)),
             pltpu.SemaphoreType.DMA((n,)),
             pltpu.SemaphoreType.DMA((n,)),
             pltpu.SemaphoreType.DMA((n,)),
             pltpu.SemaphoreType.DMA((n,)),
-            pltpu.SemaphoreType.DMA((2,)),
+            pltpu.SemaphoreType.DMA((1,)),
             pltpu.SemaphoreType.REGULAR,
         ],
         compiler_params=pltpu.CompilerParams(
             collective_id=0, has_side_effects=True, vmem_limit_bytes=60 * 1024 * 1024),
         name="regroup_analyse",
-    )(fc, obs_index, weights, readings)
-    return jnp.transpose(result, (1, 0, 2))
+    )(ensemble, flow, obs_index, obs_count[:, None], obs_dist, prec, readings)
 
 
 def solution(mesh):

time: 228 us -> 212 us (0.930)
  local copies, waits for them, and re-layouts: 14.5 us -> 4.79 us
  other arithmetic: 7.02 us -> 0 us
  Pallas kernels: 203 us -> 207 us
    transpose x1 -> x0, local copies, waits for them, and re-layouts: 6.9 us -> none  [per_device(): return jnp.transpose(result, (1, 0, 2))]
    sub x1 -> x0, other arithmetic: 6.42 us -> none  [forecast(): field - jnp.maximum(flow, 0.0) * (field - west)]
    pallas_call x1, Pallas kernels: 203 us -> 207 us  [per_device(): pl.pallas_call(functools.partial(kernel, n), out_shape=jax.ShapeDtypeStru...]
    slice x2 -> x0, local copies, waits for them, and re-layouts: 2.97 us -> none  [the longest x1 1.73 us: forecast(): east = jnp.concatenate([field[..., 1:], after], axis=2)]
    unnamed x11 -> x1, local copies, waits for them, and re-layouts: 4.68 us -> 4.79 us
  transfers between devices with their start and end apart: 2 -> 0, of which waited for: 0 -> 0; matrix products, arithmetic and copies ran while one was open for 3% -> 0% of each run, Pallas kernels for 0% -> 0%
where the time goes in v3:
time: 212 us
  Pallas kernels  207 us (98%)
  local copies, waits for them, and re-layouts  4.79 us (2%)
    pallas_call x1, Pallas kernels, per_device(): pl.pallas_call(functools.partial(kernel, n), out_shape=jax.ShapeDtypeStru...  207 us
    unnamed x1, local copies, waits for them, and re-layouts  4.79 us

profile of v3, /device:TPU:29, one launch (start us, length us, event | category | flops | bytes accessed | tf_op | source)
XLA Modules:
  0.0 212.2 jit_solution(3174430492109292100)
XLA Ops:
  0.7 206.7 %regroup_analyse.1 = f32[128,4,2048]{2,1,0:T(4,128)} custom-call(f32[128,4,2048]{2,1,0:T(4,128)} %ens.1, f32[4,2048]{1,0:T(4,128)} %flow.1, s32[1,512]{1,0:T(1,128)} %cells.1, s32[1,1]{1,0:T(1,128)} %bitcast.1.count, s32[1,512]{1,0:T(1,128)} %dist.1, f32[1,512]{1,0:T(1,128)} %prec.1, f32[1,512]{1,0:T(1,128)} %readings.1), custom_call_target="tpu_custom_call" | custom-call | tf_op jit(solution)/shard_map/regroup_analyse/pallas_call | solution.py:305
  207.4 4.8 %copy.10 = f32[128,4,2048]{2,1,0:T(4,128)} copy(f32[128,4,2048]{2,1,0:T(4,128)} %regroup_analyse.1) | data formatting | bytes 8388608

commit v4 on v3

--- a/solution.py
+++ b/solution.py
@@ -107,6 +107,16 @@
             outbuf[l, rows_of(dst), :] = (
                 centre - jnp.maximum(f, 0.0) * (centre - west) - jnp.minimum(f, 0.0) * (east - centre))
 
+    def nth(s, mine, count):
+        if count % 2:
+            return lax.rem(mine + s, count)
+        half = count // 2
+        upper = mine // half
+        outer = ((4 * mine < count) | (4 * mine >= 3 * count)).astype(jnp.int32)
+        side = lax.rem(upper + s // half + 1 - outer, 2)
+        j = lax.rem(s, half)
+        return jnp.where(side == 1, half + j, half - 1 - j)
+
     own = pltpu.make_async_copy(outbuf.at[:, rows_of(me), :], slab.at[:, rows_of(me), :], local.at[0])
     for load in inputs:
         load.wait()
@@ -128,19 +138,15 @@
         def _():
             pl.semaphore_wait(gate, 1)
 
-    def inner(s, _):
-        send_forecast(1 + lax.rem(me + s, n - 2))
-        return 0
-
-    lax.fori_loop(0, n - 2, inner, 0)
+    def serve(s, _):
+        send_forecast(nth(s, me, n))
+        return 0
+
+    early = 0 if n % 2 else n // 2 - 1
+    lax.fori_loop(0, early, serve, 0)
     for edge in halo:
         edge.wait()
-
-    def outer(s, _):
-        send_forecast(s * (n - 1))
-        return 0
-
-    lax.fori_loop(0, 2, outer, 0)
+    lax.fori_loop(early, n, serve, 0)
 
     def fill(b, _):
         at = pl.ds(pl.multiple_of(b * step, step), step)
@@ -254,7 +260,7 @@
     each = tile // group
 
     def apply(t, _):
-        b = lax.rem(me // each + 1 + t, tiles)
+        b = nth(t, me // each, tiles)
         at = pl.ds(pl.multiple_of(b * tile, tile), tile)
         value = dot(poly_a[:, at], low[...], ((0,), (0,))) + rows[0:1, :]
         for l in range(levels):

time: 212 us -> 220 us (1.038)
  the two profiles are of different devices: /device:TPU:29 before, /device:TPU:1 now
where the time goes in v4:
time: 220 us
  Pallas kernels  214 us (97%)
  local copies, waits for them, and re-layouts  4.79 us (2%)
    pallas_call x1, Pallas kernels, per_device(): pl.pallas_call(functools.partial(kernel, n), out_shape=jax.ShapeDtypeStru...  214 us
    unnamed x1, local copies, waits for them, and re-layouts  4.79 us

profile of v4, /device:TPU:1, one launch (start us, length us, event | category | flops | bytes accessed | tf_op | source)
XLA Modules:
  0.0 219.8 jit_solution(1644564136696377805)
XLA Ops:
  0.7 214.4 %regroup_analyse.1 = f32[128,4,2048]{2,1,0:T(4,128)} custom-call(f32[128,4,2048]{2,1,0:T(4,128)} %ens.1, f32[4,2048]{1,0:T(4,128)} %flow.1, s32[1,512]{1,0:T(1,128)} %cells.1, s32[1,1]{1,0:T(1,128)} %bitcast.1.count, s32[1,512]{1,0:T(1,128)} %dist.1, f32[1,512]{1,0:T(1,128)} %prec.1, f32[1,512]{1,0:T(1,128)} %readings.1), custom_call_target="tpu_custom_call" | custom-call | tf_op jit(solution)/shard_map/regroup_analyse/pallas_call | solution.py:311
  215.0 4.8 %copy.10 = f32[128,4,2048]{2,1,0:T(4,128)} copy(f32[128,4,2048]{2,1,0:T(4,128)} %regroup_analyse.1) | data formatting | bytes 8388608

commit v5 on v3

--- a/solution.py
+++ b/solution.py
@@ -128,19 +128,17 @@
         def _():
             pl.semaphore_wait(gate, 1)
 
-    def inner(s, _):
-        send_forecast(1 + lax.rem(me + s, n - 2))
-        return 0
-
-    lax.fori_loop(0, n - 2, inner, 0)
+    def nth(s):
+        return jnp.where(s < n - 2, 1 + lax.rem(me + s, n - 2), (s - (n - 2)) * (n - 1))
+
+    def serve(s, _):
+        send_forecast(nth(s))
+        return 0
+
+    lax.fori_loop(0, n - 2, serve, 0)
     for edge in halo:
         edge.wait()
-
-    def outer(s, _):
-        send_forecast(s * (n - 1))
-        return 0
-
-    lax.fori_loop(0, 2, outer, 0)
+    lax.fori_loop(n - 2, n, serve, 0)
 
     def fill(b, _):
         at = pl.ds(pl.multiple_of(b * step, step), step)
@@ -154,15 +152,22 @@
     weights = jnp.where(live, reach, 0.0)
 
     def sent(s, _):
-        there(lax.rem(me + s, n), me).wait_send()
-        return 0
-
-    lax.fori_loop(1, n, sent, 0)
+        dst = nth(s)
+
+        @pl.when(dst != me)
+        def _():
+            there(dst, me).wait_send()
+
+        return 0
+
+    lax.fori_loop(0, n // 2, sent, 0)
     if paired:
 
         @pl.when(jnp.logical_not(second_of_pair))
         def _():
             pl.semaphore_signal(gate, inc=1, device_id={"lon": partner}, device_id_type=MESH)
+
+    lax.fori_loop(n // 2, n, sent, 0)
 
     def block_sum(src):
         at = pl.ds(pl.multiple_of(src * group, group), group)

time: 212 us -> 208 us (0.981)
  Pallas kernels: 207 us -> 202 us
    pallas_call x1, Pallas kernels: 207 us -> 202 us  [per_device(): pl.pallas_call(functools.partial(kernel, n), out_shape=jax.ShapeDtypeStru...]
where the time goes in v5:
time: 208 us; the launch traced here: 207 us
  Pallas kernels  202 us (97%)
  local copies, waits for them, and re-layouts  4.79 us (2%)
    pallas_call x1, Pallas kernels, per_device(): pl.pallas_call(functools.partial(kernel, n), out_shape=jax.ShapeDtypeStru...  202 us
    unnamed x1, local copies, waits for them, and re-layouts  4.79 us

profile of v5, /device:TPU:29, one launch (start us, length us, event | category | flops | bytes accessed | tf_op | source)
XLA Modules:
  0.0 207.5 jit_solution(16275841867195812668)
XLA Ops:
  0.7 202.0 %regroup_analyse.1 = f32[128,4,2048]{2,1,0:T(4,128)} custom-call(f32[128,4,2048]{2,1,0:T(4,128)} %ens.1, f32[4,2048]{1,0:T(4,128)} %flow.1, s32[1,512]{1,0:T(1,128)} %cells.1, s32[1,1]{1,0:T(1,128)} %bitcast.1.count, s32[1,512]{1,0:T(1,128)} %dist.1, f32[1,512]{1,0:T(1,128)} %prec.1, f32[1,512]{1,0:T(1,128)} %readings.1), custom_call_target="tpu_custom_call" | custom-call | tf_op jit(solution)/shard_map/regroup_analyse/pallas_call | solution.py:310
  202.7 4.8 %copy.10 = f32[128,4,2048]{2,1,0:T(4,128)} copy(f32[128,4,2048]{2,1,0:T(4,128)} %regroup_analyse.1) | data formatting | bytes 8388608

commit v6 on v5

--- a/solution.py
+++ b/solution.py
@@ -309,9 +309,9 @@
     square = pltpu.VMEM((members, members), bf16)
     return pl.pallas_call(
         functools.partial(kernel, n),
-        out_shape=jax.ShapeDtypeStruct(ensemble.shape, f32),
+        out_shape=pltpu.VMEM(ensemble.shape, f32),
         in_specs=[hbm] + [vmem] * 6,
-        out_specs=hbm,
+        out_specs=vmem,
         scratch_shapes=[
             pltpu.VMEM((levels, group, columns + 256), f32),
             slab,
@@ -337,7 +337,7 @@
             pltpu.SemaphoreType.REGULAR,
         ],
         compiler_params=pltpu.CompilerParams(
-            collective_id=0, has_side_effects=True, vmem_limit_bytes=60 * 1024 * 1024),
+            collective_id=0, has_side_effects=True, vmem_limit_bytes=67043328 - 4 * ensemble.size - 4096),
         name="regroup_analyse",
     )(ensemble, flow, obs_index, obs_count[:, None], obs_dist, prec, readings)
 

time: 208 us -> 205 us (0.986)
  local copies, waits for them, and re-layouts: 4.79 us -> 2.02 us
    unnamed x1, local copies, waits for them, and re-layouts: 4.79 us -> 2.02 us
where the time goes in v6:
time: 205 us; the launch traced here: 204 us
  Pallas kernels  202 us (99%)
    pallas_call x1, Pallas kernels, per_device(): pl.pallas_call(functools.partial(kernel, n), out_shape=pltpu.VMEM(ensembl...  202 us

profile of v6, /device:TPU:29, one launch (start us, length us, event | category | flops | bytes accessed | tf_op | source)
XLA Modules:
  0.0 204.3 jit_solution(2970955676042640085)
XLA Ops:
  0.7 201.6 %regroup_analyse.1 = f32[128,4,2048]{2,1,0:T(4,128)S(1)} custom-call(f32[128,4,2048]{2,1,0:T(4,128)} %ens.1, f32[4,2048]{1,0:T(4,128)} %flow.1, s32[1,512]{1,0:T(1,128)} %cells.1, s32[1,1]{1,0:T(1,128)} %bitcast.1.count, s32[1,512]{1,0:T(1,128)} %dist.1, f32[1,512]{1,0:T(1,128)} %prec.1, f32[1,512]{1,0:T(1,128)} %readings.1), custom_call_target="tpu_custom_call" | custom-call | tf_op jit(solution)/shard_map/regroup_analyse/pallas_call | solution.py:310
  202.3 2.0 copy.9
